TPU v7x, 256 devices: a whole 4x4x8 slice. The times are simulated.
256 devices in a mesh: pix: 32 (over z, y), shell: 8 (over x, core).
Axes of the slice: x: 4, y: 4, z: 8, core: 2. Of those that a mesh axis runs over, the one named last changes fastest.
Arguments:
- field: float32 [128, 1048576], P('shell', 'pix'), may hold values from -3 to 3
- momentum: float32 [128, 1048576], P('shell', 'pix'), may hold values from -6 to 6
- kernels: float32 [4, 20, 128], P(None, None, 'shell'), may hold values from 0.002 to 0.02
- depth_class: int32 [1048576], P('pix'), may hold values from 0 to 3
- counts: int32 [20, 1048576], P(None, 'pix'), may hold values from 0 to 12
- mask: float32 [1048576], P('pix'), may hold values from 0.1 to 1.5, as said below
- mean_counts: float32 [20], replicated, may hold values from 1 to 8
- shell_scale: float32 [128], P('shell'), may hold values from 0.5 to 2
Outputs:
- gradient: float32 [128, 1048576], P('shell', 'pix')
- loglik: float32 [], replicated
Inputs may be any that keep to these rules, and one draw needn't show every extreme that they name: `mask`: mask weights are positive.
All inputs are finite; a program needn't handle non-finite values.
Results may differ from a plain program's by a relative error of at most 0.00005.
Values sent between devices are 32-bit elements; how exact they have to be, the bound alone decides.
No kernel may reach another device: no remote copies, remote signals or barrier semaphores. Data moves between devices by JAX's collectives and lax.ppermute only.
A program may use at most 128 MiB of HBM per device.

v0:
```python
import jax
import jax.numpy as jnp
from jax import lax
from jax.sharding import PartitionSpec as P

CYCLE = 2048
LEAP = 0.1
ANGULAR = 0.5
RADIAL = 0.5


def padded_2(cells, sides, width):
    for axis, dim in sides:
        count = lax.axis_size(axis)
        ends = count - 1
        head = lax.slice_in_dim(cells, 0, width, axis=dim)
        tail = lax.slice_in_dim(cells, cells.shape[dim] - width, cells.shape[dim], axis=dim)
        cells = jnp.concatenate(
            [
                lax.ppermute(tail, axis, [(i, (i + 1) % count) for i in range(ends)]),
                cells,
                lax.ppermute(head, axis, [((i + 1) % count, i) for i in range(ends)]),
            ],
            axis=dim,
        )
    return cells


def shards(field, momentum, kernels, depth_class, counts, mask, mean_counts, shell_scale):
    shells_here, pixels = field.shape
    classes, bins, _ = kernels.shape
    total_pix = pixels * lax.axis_size("pix")
    position = field + LEAP * momentum
    density = jnp.exp(position)
    flat = kernels.reshape(classes * bins, shells_here)
    onehot = (depth_class[None, :] == jnp.arange(classes, dtype=jnp.int32)[:, None]).astype(
        jnp.float32
    )
    every = jnp.dot(
        flat, density, precision=lax.Precision.HIGHEST, preferred_element_type=jnp.float32
    )
    partial_proj = jnp.sum(every.reshape(classes, bins, pixels) * onehot[:, None, :], axis=0)
    counted = counts.astype(jnp.float32)
    proj = lax.psum(partial_proj, "shell")
    weighted, total = lax.psum(
        (jnp.sum(mask[None, :] * proj, axis=1), jnp.sum(counted, axis=1)), "pix"
    )
    norm = weighted / total_pix
    rate = mean_counts[:, None] * mask[None, :] * proj / norm[:, None]
    local_sum = jnp.sum(counted * jnp.log(rate) - rate)
    loglik = lax.psum(local_sum, "pix") / (bins * total_pix)
    ratio = counted / proj - (total / (total_pix * norm))[:, None] * mask[None, :]
    padded = padded_2(position, (("pix", 1),), CYCLE)
    angular = (
        4.0 * position
        - padded[:, CYCLE - 1 : CYCLE - 1 + pixels]
        - padded[:, CYCLE + 1 : CYCLE + 1 + pixels]
    )
    angular = angular - padded[:, 0:pixels] - padded[:, 2 * CYCLE : 2 * CYCLE + pixels]
    stacked = padded_2(position, (("shell", 0),), 1)
    radial = 2.0 * position - stacked[:-2] - stacked[2:]
    spread = (onehot[:, None, :] * ratio[None, :, :]).reshape(classes * bins, pixels)
    back = lax.dot_general(
        flat,
        spread,
        (((0,), (0,)), ((), ())),
        precision=lax.Precision.HIGHEST,
        preferred_element_type=jnp.float32,
    )
    like = density * back
    gradient = (
        like
        - position / (shell_scale[:, None] * shell_scale[:, None])
        - ANGULAR * angular
        - RADIAL * radial
    )
    return (gradient, loglik)


def solution(mesh):
    placed = (
        P("shell", "pix"),
        P("shell", "pix"),
        P(None, None, "shell"),
        P("pix"),
        P(None, "pix"),
        P("pix"),
        P(),
        P("shell"),
    )
    return jax.shard_map(
        shards, mesh=mesh, in_specs=placed, out_specs=(P("shell", "pix"), P()), check_vma=False
    )
```

profile of v0, /device:TPU:8, one launch (start us, length us, event | category | flops | bytes accessed | tf_op | source)
XLA Modules:
  0.0 298.6 jit_solution(3591351216382486892)
XLA Ops:
  7.2 0.0 all-reduce.3.cloned.1.call-start
  7.2 0.8 copy.10
  8.0 0.1 reshape.36
  8.1 2.5 multiply_add_fusion
  10.5 0.0 copy-start.1
  10.5 10.9 %convolution_bitcast_fusion = f32[80,32768]{1,0:T(8,128)} fusion(f32[80,16]{0,1:T(8,128)S(1)} %reshape.36, f32[16,32768]{1,0:T(8,128)S(1)} %multiply_add_fusion), kind=kOutput, calls=%fused_computation | convolution fusion | flops 503316480 | bytes 12588032 | tf_op jit(solution)/shard_map/dot_general | solution.py:39
  21.4 0.0 copy-start.4
  21.4 11.4 %reshape.37 = f32[4,20,32768]{2,1,0:T(8,128)} reshape(f32[80,32768]{1,0:T(8,128)} %convolution_bitcast_fusion) | data formatting | bytes 20971520 | tf_op jit(solution)/shard_map/reshape | solution.py:42
  32.8 0.0 copy-done.4
  32.8 0.1 fusion.20
  32.9 0.0 copy-start.2
  32.9 0.8 copy-done.2
  33.7 8.0 %multiply_reduce_fusion = f32[20,32768]{1,0:T(8,128)} fusion(f32[4,20,32768]{2,1,0:T(8,128)} %reshape.37, f32[4,32768]{1,0:T(4,128)S(1)} %fusion.20), kind=kLoop, calls=%fused_computation.5 | loop fusion | flops 4587520 | bytes 13631488 | tf_op jit(solution)/shard_map/reduce_sum | solution.py:42
  41.7 0.0 copy-start.3
  41.7 0.0 all-reduce.3.cloned.1.call-update
  41.8 0.0 copy-start.6
  41.8 0.0 copy-start.5
  41.8 3.6 %collective-permute-start = (f32[16,2048]{1,0:T(8,128)S(1)}, f32[16,2048]{1,0:T(8,128)}, u32[]{:S(2)}, u32[]{:S(2)}) collective-permute-start(f32[16,2048]{1,0:T(8,128)S(1)} %get-tuple-element.8), channel_id=1, source_target_pairs={{0,8},{8,16},{16,24},{24,32},{32,40},{40,48},{48,56},{56,64},{64,7... | collective-permute-start | bytes 393224 | tf_op jit(solution)/shard_map/ppermute | solution.py:20
  45.4 3.0 %collective-permute-start.1 = (f32[16,2048]{1,0:T(8,128)S(1)}, f32[16,2048]{1,0:T(8,128)}, u32[]{:S(2)}, u32[]{:S(2)}) collective-permute-start(f32[16,2048]{1,0:T(8,128)S(1)} %get-tuple-element.9), channel_id=1, source_target_pairs={{8,0},{16,8},{24,16},{32,24},{40,32},{48,40},{56,48},{64,56},{72,6... | collective-permute-start | bytes 393224 | tf_op jit(solution)/shard_map/ppermute | solution.py:22
  48.4 0.0 copy-done.1
  48.5 0.9 fusion.21
  49.3 1.9 collective-permute-start.2
  51.3 1.3 collective-permute-start.3
  52.6 66.3 %all-reduce.3.cloned.1.call-done = f32[20,32768]{1,0:T(8,128)} async-done(((f32[20,32768]{1,0:T(8,128)}), f32[20,32768]{1,0:T(8,128)}) %all-reduce.3.cloned.1.call-update) | async-done | bytes 2621456 | tf_op jit(solution)/shard_map/psum | solution.py:44
  118.9 0.0 copy-done.3
  118.9 0.0 copy-start
  118.9 2.4 multiply_reduce_fusion.1
  121.3 0.0 copy-done.6
  121.3 71.1 %psum.30 = f32[20]{0:T(128)S(1)} all-reduce(f32[20]{0:T(128)S(1)} %multiply_reduce_fusion.1), channel_id=1, replica_groups=mesh['pix'=32,'shell'=8] {'pix'}, use_global_device_ids=true, to_apply=%region_5.0 | all-reduce | flops 20 | bytes 160 | tf_op jit(solution)/shard_map/psum | solution.py:45
  192.5 0.0 copy-done.5
  192.5 0.0 copy-done
  192.5 3.6 %subtract_reduce_fusion = (f32[]{:T(128)}, f32[20]{0:T(128)S(1)}) fusion(f32[20,32768]{1,0:T(8,128)S(1)} %copy-done, s32[20,32768]{1,0:T(8,128)} %param.12, f32[20]{0:T(128)S(1)} %broadcast_multiply_fusion, f32[20]{0:T(128)S(1)} %copy-done.5, f32[32768]{0:T(1024)S(1)} %copy-done.3), kind=kLoop, calls=%fused_computation.8 | loop fusion | flops 5242859 | bytes 5374196 | tf_op jit(solution)/shard_map/reduce_sum | solution.py:50
  196.1 74.9 %all-reduce = (f32[20]{0:T(128)S(1)}, f32[]{:T(128)}) all-reduce(f32[20]{0:T(128)S(1)} %get-tuple-element.3, f32[]{:T(128)} %get-tuple-element.2), channel_id=1, replica_groups=mesh['pix'=32,'shell'=8] {'pix'}, use_global_device_ids=true, to_apply=%region_3.0 | all-reduce | flops 21 | bytes 168 | tf_op jit(solution)/shard_map/psum | solution.py:45
  271.1 4.1 %multiply_subtract_fusion = f32[20,32768]{1,0:T(8,128)} fusion(f32[20,32768]{1,0:T(8,128)S(1)} %copy-done, s32[20,32768]{1,0:T(8,128)} %param.12, f32[20]{0:T(128)S(1)} %div.29, f32[32768]{0:T(1024)S(1)} %copy-done.3), kind=kLoop, calls=%fused_computation.9 | loop fusion | flops 2621440 | bytes 7995472 | tf_op jit(solution)/shard_map/sub | solution.py:52
  275.8 0.0 collective-permute-done
  275.8 0.0 collective-permute-done.1
  275.8 0.0 collective-permute-done.2
  275.8 0.0 collective-permute-done.3
  275.9 14.8 %fusion.11 = f32[16,32768]{1,0:T(8,128)} fusion(f32[16,32768]{1,0:T(8,128)} %copy-done.1, f32[16,2048]{1,0:T(8,128)} %collective-permute-done.1, f32[16,2048]{1,0:T(8,128)} %collective-permute-done, f32[1,32768]{1,0:T(1,128)} %collective-permute-done.3, f32[1,32768]{1,0:T(1,128)} %collective-permute-done.2, f32[4,20,16]{1,2,0:T(8,128)} %param.10, ...), kind=kOutput, calls=%fused_computation.22 | convolution fusion | flops 516947968 | bytes 7869504 | tf_op jit(solution)/shard_map/dot_general | solution.py:63
  (4 shorter events, 0.0 us)
Async XLA Ops:
  7.2 111.7 %all-reduce.3.cloned.1.call-start = ((), (), s32[]{:S(2)}) async-start(), calls=%async_computation | async-start | bytes 6291456 | tf_op jit(solution)/shard_map/psum | solution.py:44
  10.5 37.9 %copy-start.1 = (f32[16,32768]{1,0:T(8,128)}, f32[16,32768]{1,0:T(8,128)S(1)}, u32[]{:S(2)}) copy-start(f32[16,32768]{1,0:T(8,128)S(1)} %multiply_add_fusion) | copy-start | bytes 6291460
  21.4 11.4 %copy-start.4 = (s32[32768]{0:T(1024)S(1)}, s32[32768]{0:T(1024)}, u32[]{:S(2)}) copy-start(s32[32768]{0:T(1024)} %param.11) | copy-start | bytes 393220
  32.9 0.8 copy-start.2
  41.7 77.2 %copy-start.3 = (f32[32768]{0:T(1024)S(1)}, f32[32768]{0:T(1024)}, u32[]{:S(2)}) copy-start(f32[32768]{0:T(1024)} %param.13) | copy-start | bytes 393220
  41.8 79.6 %copy-start.6 = (f32[16]{0:T(128)S(1)}, f32[16]{0:T(128)}, u32[]{:S(2)}) copy-start(f32[16]{0:T(128)} %param.15) | copy-start | bytes 196
  41.8 150.7 %copy-start.5 = (f32[20]{0:T(128)S(1)}, f32[20]{0:T(128)}, u32[]{:S(2)}) copy-start(f32[20]{0:T(128)} %param.14) | copy-start | bytes 244
  41.8 234.0 %collective-permute-start = (f32[16,2048]{1,0:T(8,128)S(1)}, f32[16,2048]{1,0:T(8,128)}, u32[]{:S(2)}, u32[]{:S(2)}) collective-permute-start(f32[16,2048]{1,0:T(8,128)S(1)} %get-tuple-element.8), channel_id=1, source_target_pairs={{0,8},{8,16},{16,24},{24,32},{32,40},{40,48},{48,56},{56,64},{64,7... | collective-permute-start | bytes 393224 | tf_op jit(solution)/shard_map/ppermute | solution.py:20
  45.4 230.4 %collective-permute-start.1 = (f32[16,2048]{1,0:T(8,128)S(1)}, f32[16,2048]{1,0:T(8,128)}, u32[]{:S(2)}, u32[]{:S(2)}) collective-permute-start(f32[16,2048]{1,0:T(8,128)S(1)} %get-tuple-element.9), channel_id=1, source_target_pairs={{8,0},{16,8},{24,16},{32,24},{40,32},{48,40},{56,48},{64,56},{72,6... | collective-permute-start | bytes 393224 | tf_op jit(solution)/shard_map/ppermute | solution.py:22
  49.3 226.5 %collective-permute-start.2 = (f32[1,32768]{1,0:T(1,128)}, f32[1,32768]{1,0:T(1,128)}, u32[]{:S(2)}, u32[]{:S(2)}) collective-permute-start(f32[1,32768]{1,0:T(1,128)} %get-tuple-element.6), channel_id=1, source_target_pairs={{0,1},{1,2},{2,3},{3,4},{4,5},{5,6},{6,7},{8,9},{9,10},{10,11},{11... | collective-permute-start | bytes 393224 | tf_op jit(solution)/shard_map/ppermute | solution.py:20
  51.3 224.6 %collective-permute-start.3 = (f32[1,32768]{1,0:T(1,128)}, f32[1,32768]{1,0:T(1,128)}, u32[]{:S(2)}, u32[]{:S(2)}) collective-permute-start(f32[1,32768]{1,0:T(1,128)} %get-tuple-element.7), channel_id=1, source_target_pairs={{1,0},{2,1},{3,2},{4,3},{5,4},{6,5},{7,6},{9,8},{10,9},{11,10},{12... | collective-permute-start | bytes 393224 | tf_op jit(solution)/shard_map/ppermute | solution.py:22
  118.9 73.6 %copy-start = (f32[20,32768]{1,0:T(8,128)S(1)}, f32[20,32768]{1,0:T(8,128)}, u32[]{:S(2)}) copy-start(f32[20,32768]{1,0:T(8,128)} %all-reduce.3.cloned.1.call-done) | copy-start | bytes 7864324
Sparse Core Ops, SparseCore 0:
  41.9 76.9 all-reduce.2
where the time goes:
time: 299 us
  blocking collectives  146 us (49%)
  waiting for transfers between devices  66.4 us (22%)
  matrix products  25.7 us (9%)
  other arithmetic  20.8 us (7%)
  between operations  15.9 us (5%)
  local copies, waits for them, and re-layouts  14 us (5%)
  starting transfers between devices  9.87 us (3%)
    psum x2, blocking collectives, shards(): lax.psum((jnp.sum(mask[None, :] * proj, axis=1), jnp.sum(counted, axis=1)...  146 us
    psum x1, waiting for transfers between devices, shards(): proj = lax.psum(partial_proj, 'shell')  66.3 us
    dot_general x1, matrix products, shards(): lax.dot_general(flat, spread, (((0,), (0,)), ((), ())), precision=lax.Pre...  14.8 us
    reshape x1, local copies, waits for them, and re-layouts, shards(): every.reshape(classes, bins, pixels) * onehot[:, None, :]  11.4 us
    dot_general x1, matrix products, shards(): jnp.dot(flat, density, precision=lax.Precision.HIGHEST, preferred_element...  10.9 us
    reduce_sum x1, other arithmetic, shards(): jnp.sum(every.reshape(classes, bins, pixels) * onehot[:, None, :], axis=0)  8.02 us
  transfers between devices with their start and end apart: 5, of which 1 were waited for; matrix products, arithmetic and copies ran while one was open for 4% of the time, Pallas kernels for 0%

commit v1 on v0

--- a/solution.py
+++ b/solution.py
@@ -41,7 +41,7 @@
     )
     partial_proj = jnp.sum(every.reshape(classes, bins, pixels) * onehot[:, None, :], axis=0)
     counted = counts.astype(jnp.float32)
-    proj = lax.psum(partial_proj, "shell")
+    proj = jnp.sum(lax.all_gather(partial_proj, "shell"), axis=0)
     weighted, total = lax.psum(
         (jnp.sum(mask[None, :] * proj, axis=1), jnp.sum(counted, axis=1)), "pix"
     )

time: 299 us -> 355 us (1.19)
  waiting for transfers between devices: 66.4 us -> 115 us
  other arithmetic: 20.8 us -> 28.3 us
    all_gather x0 -> x1, waiting for transfers between devices: none -> 115 us  [shards(): proj = jnp.sum(lax.all_gather(partial_proj, 'shell'), axis=0)]
    psum x1 -> x0, waiting for transfers between devices: 66.3 us -> none  [shards(): proj = lax.psum(partial_proj, 'shell')]
    reduce_sum x0 -> x1, other arithmetic: none -> 9.46 us  [shards(): proj = jnp.sum(lax.all_gather(partial_proj, 'shell'), axis=0)]
  transfers between devices with their start and end apart: 5 -> 5, of which waited for: 1 -> 1; matrix products, arithmetic and copies ran while one was open for 4% -> 5% of each run, Pallas kernels for 0% -> 0%
where the time goes in v1:
time: 355 us; the launch traced here: 354 us
  blocking collectives  146 us (41%)
  waiting for transfers between devices  115 us (32%)
  other arithmetic  28.3 us (8%)
  matrix products  25.8 us (7%)
  between operations  15.9 us (4%)
  local copies, waits for them, and re-layouts  13.4 us (4%)
  starting transfers between devices  9.87 us (3%)
    psum x2, blocking collectives, shards(): lax.psum((jnp.sum(mask[None, :] * proj, axis=1), jnp.sum(counted, axis=1)...  146 us
    all_gather x1, waiting for transfers between devices, shards(): proj = jnp.sum(lax.all_gather(partial_proj, 'shell'), axis=0)  115 us
    dot_general x1, matrix products, shards(): lax.dot_general(flat, spread, (((0,), (0,)), ((), ())), precision=lax.Pre...  15 us
    reshape x1, local copies, waits for them, and re-layouts, shards(): every.reshape(classes, bins, pixels) * onehot[:, None, :]  11.4 us
    dot_general x1, matrix products, shards(): jnp.dot(flat, density, precision=lax.Precision.HIGHEST, preferred_element...  10.9 us
    reduce_sum x1, other arithmetic, shards(): proj = jnp.sum(lax.all_gather(partial_proj, 'shell'), axis=0)  9.46 us
    reduce_sum x1, other arithmetic, shards(): jnp.sum(every.reshape(classes, bins, pixels) * onehot[:, None, :], axis=0)  8.11 us
  transfers between devices with their start and end apart: 5, of which 1 were waited for; matrix products, arithmetic and copies ran while one was open for 5% of the time, Pallas kernels for 0%

profile of v1, /device:TPU:8, one launch (start us, length us, event | category | flops | bytes accessed | tf_op | source)
XLA Modules:
  0.0 354.4 jit_solution(8711617326727077758)
XLA Ops:
  7.2 0.0 all-gather.4.cloned.1.call-start
  7.2 0.8 copy.11
  8.0 0.1 reshape.36
  8.1 2.5 multiply_add_fusion
  10.5 0.0 copy-start
  10.5 10.9 %convolution_bitcast_fusion = f32[80,32768]{1,0:T(8,128)} fusion(f32[80,16]{0,1:T(8,128)S(1)} %reshape.36, f32[16,32768]{1,0:T(8,128)S(1)} %multiply_add_fusion), kind=kOutput, calls=%fused_computation | convolution fusion | flops 503316480 | bytes 12588032 | tf_op jit(solution)/shard_map/dot_general | solution.py:39
  21.4 0.0 copy-start.3
  21.4 11.4 %reshape.37 = f32[4,20,32768]{2,1,0:T(8,128)} reshape(f32[80,32768]{1,0:T(8,128)} %convolution_bitcast_fusion) | data formatting | bytes 20971520 | tf_op jit(solution)/shard_map/reshape | solution.py:42
  32.8 0.0 copy-done.3
  32.8 0.1 fusion.20
  32.9 0.0 copy-start.1
  32.9 8.1 %multiply_reduce_fusion = f32[20,32768]{1,0:T(8,128)} fusion(f32[4,20,32768]{2,1,0:T(8,128)} %reshape.37, f32[4,32768]{1,0:T(4,128)S(1)} %fusion.20), kind=kLoop, calls=%fused_computation.5 | loop fusion | flops 4587520 | bytes 13631488 | tf_op jit(solution)/shard_map/reduce_sum | solution.py:42
  41.0 0.0 copy-done.1
  41.0 0.0 all-gather.4.cloned.1.call-update
  41.1 3.5 collective-permute-start
  44.6 3.0 collective-permute-start.1
  47.6 0.0 copy-done
  47.6 0.9 fusion.21
  48.5 1.9 collective-permute-start.2
  50.4 0.0 copy-start.2
  50.4 1.4 collective-permute-start.3
  51.8 115.0 %all-gather.4.cloned.1.call-done = f32[8,20,32768]{2,1,0:T(8,128)} async-done(((f32[1,20,32768]{2,1,0:T(8,128)}), f32[8,20,32768]{2,1,0:T(8,128)}) %all-gather.4.cloned.1.call-update) | async-done | bytes 20971536 | tf_op jit(solution)/shard_map/all_gather | solution.py:44
  166.8 9.5 %reduce_sum.46 = f32[20,32768]{1,0:T(8,128)S(1)} reduce(f32[8,20,32768]{2,1,0:T(8,128)} %all-gather.4.cloned.1.call-done, f32[]{:T(128)} %constant.4.clone.1), dimensions={0}, to_apply=%region_1.0 | reduce | flops 4587520 | bytes 23592964 | tf_op jit(solution)/shard_map/reduce_sum | solution.py:44
  176.3 0.0 copy-done.2
  176.3 0.0 copy-start.5
  176.3 0.0 copy-start.4
  176.3 0.4 multiply_reduce_fusion.1
  176.8 0.2 copy-done.5
  177.0 71.1 %psum.22 = f32[20]{0:T(128)S(1)} all-reduce(f32[20]{0:T(128)S(1)} %multiply_reduce_fusion.1), channel_id=1, replica_groups=mesh['pix'=32,'shell'=8] {'pix'}, use_global_device_ids=true, to_apply=%region_5.0 | all-reduce | flops 20 | bytes 160 | tf_op jit(solution)/shard_map/psum | solution.py:45
  248.1 0.0 copy-done.4
  248.1 3.6 %subtract_reduce_fusion = (f32[]{:T(128)}, f32[20]{0:T(128)S(1)}) fusion(f32[20,32768]{1,0:T(8,128)S(1)} %reduce_sum.46, s32[20,32768]{1,0:T(8,128)} %param.12, f32[20]{0:T(128)S(1)} %broadcast_multiply_fusion, f32[20]{0:T(128)S(1)} %copy-done.4, f32[32768]{0:T(1024)S(1)} %copy-done.2), kind=kLoop, calls=%fused_computation.8 | loop fusion | flops 5242859 | bytes 5374196 | tf_op jit(solution)/shard_map/reduce_sum | solution.py:50
  251.8 74.9 %all-reduce = (f32[20]{0:T(128)S(1)}, f32[]{:T(128)}) all-reduce(f32[20]{0:T(128)S(1)} %get-tuple-element.3, f32[]{:T(128)} %get-tuple-element.2), channel_id=1, replica_groups=mesh['pix'=32,'shell'=8] {'pix'}, use_global_device_ids=true, to_apply=%region_3.0 | all-reduce | flops 21 | bytes 168 | tf_op jit(solution)/shard_map/psum | solution.py:45
  326.7 4.1 %multiply_subtract_fusion = f32[20,32768]{1,0:T(8,128)} fusion(f32[20,32768]{1,0:T(8,128)S(1)} %reduce_sum.46, s32[20,32768]{1,0:T(8,128)} %param.12, f32[20]{0:T(128)S(1)} %div.29, f32[32768]{0:T(1024)S(1)} %copy-done.2), kind=kLoop, calls=%fused_computation.9 | loop fusion | flops 2621440 | bytes 7995472 | tf_op jit(solution)/shard_map/sub | solution.py:52
  331.5 0.0 collective-permute-done
  331.5 0.0 collective-permute-done.1
  331.5 0.0 collective-permute-done.2
  331.5 0.0 collective-permute-done.3
  331.5 15.0 %fusion.11 = f32[16,32768]{1,0:T(8,128)} fusion(f32[16,32768]{1,0:T(8,128)} %copy-done, f32[16,2048]{1,0:T(8,128)} %collective-permute-done.1, f32[16,2048]{1,0:T(8,128)} %collective-permute-done, f32[1,32768]{1,0:T(1,128)} %collective-permute-done.3, f32[1,32768]{1,0:T(1,128)} %collective-permute-done.2, f32[4,20,16]{1,2,0:T(8,128)} %param.10, ...), kind=kOutput, calls=%fused_computation.22 | convolution fusion | flops 516947968 | bytes 7869504 | tf_op jit(solution)/shard_map/dot_general | solution.py:63
  (4 shorter events, 0.0 us)
Async XLA Ops:
  7.2 159.7 %all-gather.4.cloned.1.call-start = ((), (), s32[]{:S(2)}) async-start(), calls=%async_computation | async-start | bytes 28311552 | tf_op jit(solution)/shard_map/all_gather | solution.py:44
  10.5 37.1 %copy-start = (f32[16,32768]{1,0:T(8,128)}, f32[16,32768]{1,0:T(8,128)S(1)}, u32[]{:S(2)}) copy-start(f32[16,32768]{1,0:T(8,128)S(1)} %multiply_add_fusion) | copy-start | bytes 6291460
  21.4 11.4 %copy-start.3 = (s32[32768]{0:T(1024)S(1)}, s32[32768]{0:T(1024)}, u32[]{:S(2)}) copy-start(s32[32768]{0:T(1024)} %param.11) | copy-start | bytes 393220
  32.9 8.1 %copy-start.1 = (f32[4,32768]{1,0:T(4,128)}, f32[4,32768]{1,0:T(4,128)S(1)}, u32[]{:S(2)}) copy-start(f32[4,32768]{1,0:T(4,128)S(1)} %fusion.20) | copy-start | bytes 1572868
  41.1 290.4 %collective-permute-start = (f32[16,2048]{1,0:T(8,128)S(1)}, f32[16,2048]{1,0:T(8,128)}, u32[]{:S(2)}, u32[]{:S(2)}) collective-permute-start(f32[16,2048]{1,0:T(8,128)S(1)} %get-tuple-element.8), channel_id=1, source_target_pairs={{0,8},{8,16},{16,24},{24,32},{32,40},{40,48},{48,56},{56,64},{64,7... | collective-permute-start | bytes 393224 | tf_op jit(solution)/shard_map/ppermute | solution.py:20
  44.6 286.9 %collective-permute-start.1 = (f32[16,2048]{1,0:T(8,128)S(1)}, f32[16,2048]{1,0:T(8,128)}, u32[]{:S(2)}, u32[]{:S(2)}) collective-permute-start(f32[16,2048]{1,0:T(8,128)S(1)} %get-tuple-element.9), channel_id=1, source_target_pairs={{8,0},{16,8},{24,16},{32,24},{40,32},{48,40},{56,48},{64,56},{72,6... | collective-permute-start | bytes 393224 | tf_op jit(solution)/shard_map/ppermute | solution.py:22
  48.5 283.0 %collective-permute-start.2 = (f32[1,32768]{1,0:T(1,128)}, f32[1,32768]{1,0:T(1,128)}, u32[]{:S(2)}, u32[]{:S(2)}) collective-permute-start(f32[1,32768]{1,0:T(1,128)} %get-tuple-element.6), channel_id=1, source_target_pairs={{0,1},{1,2},{2,3},{3,4},{4,5},{5,6},{6,7},{8,9},{9,10},{10,11},{11... | collective-permute-start | bytes 393224 | tf_op jit(solution)/shard_map/ppermute | solution.py:20
  50.4 125.9 %copy-start.2 = (f32[32768]{0:T(1024)S(1)}, f32[32768]{0:T(1024)}, u32[]{:S(2)}) copy-start(f32[32768]{0:T(1024)} %param.13) | copy-start | bytes 393220
  50.4 281.1 %collective-permute-start.3 = (f32[1,32768]{1,0:T(1,128)}, f32[1,32768]{1,0:T(1,128)}, u32[]{:S(2)}, u32[]{:S(2)}) collective-permute-start(f32[1,32768]{1,0:T(1,128)} %get-tuple-element.7), channel_id=1, source_target_pairs={{1,0},{2,1},{3,2},{4,3},{5,4},{6,5},{7,6},{9,8},{10,9},{11,10},{12... | collective-permute-start | bytes 393224 | tf_op jit(solution)/shard_map/ppermute | solution.py:22
  176.3 0.7 copy-start.5
  176.3 71.8 %copy-start.4 = (f32[20]{0:T(128)S(1)}, f32[20]{0:T(128)}, u32[]{:S(2)}) copy-start(f32[20]{0:T(128)} %param.14) | copy-start | bytes 244
Sparse Core Ops, SparseCore 0:
  41.2 125.6 all-gather.3
